TPU v7x, 512 devices: a whole 4x4x16 slice. The times are simulated.
512 devices in a mesh: sx: 32 (over z_hi, y, core), sy: 16 (over x, z_lo).
Axes of the slice: x: 4, y: 4, z: 16 (z_hi: 4, z_lo: 4; z = z_hi * 4 + z_lo), core: 2. Of those that a mesh axis runs over, the one named last changes fastest.
Arguments:
- forward_prop: bfloat16 [2, 2, 12, 12, 64, 4096], P(None, None, None, None, 'sx', 'sy'), may hold values from -0.08984375 to 0.08984375
- backward_prop: bfloat16 [2, 2, 12, 12, 64, 4096], P(None, None, None, None, 'sx', 'sy'), may hold values from -0.08984375 to 0.08984375
- gamma_table: int32 [16, 4, 2], replicated, may hold values from 0 to 3, as said below
- source_site: int32 [3], replicated, may hold values from 0 to 63
- momenta: int32 [32, 3], replicated, may hold values from -8 to 7
Outputs:
- corr: float32 [16, 2, 2, 64, 4096], P(None, None, None, 'sx', 'sy')
- listed: float32 [2, 16, 2, 32], replicated
Inputs may be any that keep to these rules, and one draw needn't show every extreme that they name: For every insertion g, gamma_table[g, 0..3, 0] is a permutation of 0..3; gamma_table[g, s, 1] is the power of i of that entry.
All inputs are finite; a program needn't handle non-finite values.
Results may differ from a plain program's by a relative error of at most 0.0003.
Values sent between devices are 32-bit elements; how exact they have to be, the bound alone decides.
A program may use at most 64 MiB of HBM per device.

v0:
```python
import math
import jax
import jax.numpy as jnp
from jax import lax
from jax.sharding import PartitionSpec as P

L = 64
LZ = 64
HIGHEST = lax.Precision.HIGHEST


def gamma_matrices(gamma_table):
    inserts = gamma_table.shape[0]
    columns = gamma_table[:, :, 0]
    powers = gamma_table[:, :, 1]
    spin_ids = jnp.arange(4, dtype=jnp.int32)
    matches = (columns[:, :, None] == spin_ids[None, None, :]).astype(jnp.float32)
    unit_re = (powers == 0).astype(jnp.float32) - (powers == 2).astype(jnp.float32)
    unit_im = (powers == 1).astype(jnp.float32) - (powers == 3).astype(jnp.float32)
    return (
        (matches * unit_re[:, :, None]).reshape(inserts, 16),
        (matches * unit_im[:, :, None]).reshape(inserts, 16),
    )


def dft_table(length, anchor):
    wavenum = jnp.arange(length, dtype=jnp.int32)
    offsets = jnp.mod(wavenum - anchor, length)
    phase_index = jnp.mod(offsets[:, None] * wavenum[None, :], length)
    angles = 2.0 * math.pi / length * phase_index.astype(jnp.float32)
    return (jnp.cos(angles), -jnp.sin(angles))


def complex_step(real_part, imag_part, table_re, table_im, pattern):
    out_re = jnp.einsum(pattern, real_part, table_re, precision=HIGHEST) - jnp.einsum(
        pattern, imag_part, table_im, precision=HIGHEST
    )
    out_im = jnp.einsum(pattern, real_part, table_im, precision=HIGHEST) + jnp.einsum(
        pattern, imag_part, table_re, precision=HIGHEST
    )
    return (out_re, out_im)


def transform(fields, source_site):
    table_re, table_im = dft_table(fields.shape[4], source_site[2])
    along_z = jnp.stack(
        complex_step(fields[:, 0], fields[:, 1], table_re, table_im, "nabz,zk->nabk"), 1
    )
    depth_share = along_z.shape[4] // lax.axis_size("sy")
    first_depth = lax.axis_index("sy") * depth_share
    length_y = along_z.shape[3] * lax.axis_size("sy")
    full_re, full_im = dft_table(length_y, source_site[1])
    part = lax.dynamic_slice_in_dim(
        lax.all_gather(along_z, "sy", axis=3, tiled=True), first_depth, depth_share, 4
    )
    step_re, step_im = complex_step(part[:, 0], part[:, 1], full_re, full_im, "nayc,yk->nakc")
    along_y = jnp.stack([step_re, step_im], 1)
    arrived = lax.all_to_all(along_y, "sx", split_axis=3, concat_axis=2, tiled=True)
    table_re, table_im = dft_table(arrived.shape[2], source_site[0])
    along_x = complex_step(arrived[:, 0], arrived[:, 1], table_re, table_im, "nxbc,xk->nbck")
    return jnp.stack(along_x, 1)


def apply_gammas(mat_re, mat_im, real_part, imag_part):
    extent = real_part.shape
    flat_re = real_part.reshape(extent[0], -1)
    flat_im = imag_part.reshape(extent[0], -1)
    out_re = jnp.dot(mat_re, flat_re, precision=HIGHEST) - jnp.dot(
        mat_im, flat_im, precision=HIGHEST
    )
    out_im = jnp.dot(mat_re, flat_im, precision=HIGHEST) + jnp.dot(
        mat_im, flat_re, precision=HIGHEST
    )
    return (out_re.reshape(extent), out_im.reshape(extent))


def project_sites(fields, source_site, momenta, rows_x, rows_y, length, depth):
    coord_x = lax.axis_index("sx") * rows_x + jnp.arange(rows_x, dtype=jnp.int32) - source_site[0]
    coord_y = lax.axis_index("sy") * rows_y + jnp.arange(rows_y, dtype=jnp.int32) - source_site[1]
    coord_z = jnp.arange(depth, dtype=jnp.int32) - source_site[2]
    part_x = jnp.mod(momenta[:, 0:1] * coord_x[None, :], length)
    part_y = jnp.mod(momenta[:, 1:2] * coord_y[None, :], length)
    part_z = jnp.mod(momenta[:, 2:3] * coord_z[None, :], depth)
    plane = jnp.mod(part_x[:, :, None] + part_y[:, None, :], length).astype(jnp.float32)
    angles = (
        2.0 * math.pi / length * plane[:, :, :, None]
        + 2.0 * math.pi / depth * part_z.astype(jnp.float32)[:, None, None, :]
    )
    angles = angles.reshape(momenta.shape[0], -1)
    cosine = jnp.cos(angles)
    sine = jnp.sin(angles)
    field_re = fields[:, 0].reshape(fields.shape[0], -1)
    field_im = fields[:, 1].reshape(fields.shape[0], -1)
    local_re = jnp.dot(field_re, cosine.T, precision=HIGHEST) + jnp.dot(
        field_im, sine.T, precision=HIGHEST
    )
    local_im = jnp.dot(field_im, cosine.T, precision=HIGHEST) - jnp.dot(
        field_re, sine.T, precision=HIGHEST
    )
    return (local_re, local_im)


def body(forward_prop, backward_prop, gamma_table, source_site, momenta):
    slices = forward_prop.shape[0]
    rows_x = forward_prop.shape[4]
    rows_y = backward_prop.shape[5] // LZ
    inserts = gamma_table.shape[0]
    forward = forward_prop.reshape(slices, 2, 4, 3, 12, -1)
    backward = backward_prop.reshape(slices, 2, 4, 3, 12, -1)
    pattern = "tscjn,tucjn->sutn"
    pair_re = jnp.einsum(
        pattern, backward[:, 0], forward[:, 0], preferred_element_type=jnp.float32
    ) + jnp.einsum(pattern, backward[:, 1], forward[:, 1], preferred_element_type=jnp.float32)
    pair_im = jnp.einsum(
        pattern, backward[:, 0], forward[:, 1], preferred_element_type=jnp.float32
    ) - jnp.einsum(pattern, backward[:, 1], forward[:, 0], preferred_element_type=jnp.float32)
    pair_re = pair_re.reshape(16, slices, -1)
    pair_im = pair_im.reshape(16, slices, -1)
    mat_re, mat_im = gamma_matrices(gamma_table)
    field_re, field_im = apply_gammas(mat_re, mat_im, pair_re, pair_im)
    fields = jnp.stack([field_re, field_im], 2).reshape(inserts * slices, 2, rows_x, rows_y, LZ)
    spectrum = transform(fields, source_site)
    local_re, local_im = project_sites(fields, source_site, momenta, rows_x, rows_y, L, LZ)
    listed_re, listed_im = lax.psum((local_re, local_im), ("sx", "sy"))
    listed_re = listed_re.reshape(inserts, slices, -1)
    listed_im = listed_im.reshape(inserts, slices, -1)
    corr_re = spectrum[:, 0].reshape(inserts, slices, spectrum.shape[2], -1)
    corr_im = spectrum[:, 1].reshape(inserts, slices, spectrum.shape[2], -1)
    return (jnp.stack([corr_re, corr_im], 2), jnp.stack([listed_re, listed_im], 0))


def solution(mesh):
    placed = (
        P(None, None, None, None, "sx", "sy"),
        P(None, None, None, None, "sx", "sy"),
        P(),
        P(),
        P(),
    )
    return jax.shard_map(
        body,
        mesh=mesh,
        in_specs=placed,
        out_specs=(P(None, None, None, "sx", "sy"), P()),
        check_vma=False,
    )
```

profile of v0, /device:TPU:1, one launch (start us, length us, event | category | flops | bytes accessed | tf_op | source)
XLA Modules:
  0.0 323.4 jit_solution(12954592644119887692)
XLA Ops:
  7.2 0.7 fusion.92
  7.9 2.1 reshape.371
  10.0 0.8 fusion.144
  10.9 4.5 %copy.82 = bf16[2,1,4,3,12,512]{4,2,3,5,0,1:T(4,128)(2,1)S(1)} copy(bf16[2,1,4,3,12,512]{5,4,3,2,1,0:T(8,128)(2,1)} %get-tuple-element.11) | data formatting | bytes 589824
  15.3 2.8 reshape.372
  18.1 2.1 fusion.145
  20.2 5.3 %copy.83 = bf16[2,1,4,3,12,512]{4,2,3,5,0,1:T(4,128)(2,1)} copy(bf16[2,1,4,3,12,512]{5,4,3,2,1,0:T(8,128)(2,1)} %get-tuple-element.13) | data formatting | bytes 589824
  25.4 3.8 %copy.80 = bf16[2,1,4,3,12,512]{4,2,3,5,0,1:T(4,128)(2,1)} copy(bf16[2,1,4,3,12,512]{5,4,3,2,1,0:T(8,128)(2,1)S(1)} %get-tuple-element.10) | data formatting | bytes 589824
  29.2 5.3 %copy.81 = bf16[2,1,4,3,12,512]{4,2,3,5,0,1:T(4,128)(2,1)} copy(bf16[2,1,4,3,12,512]{5,4,3,2,1,0:T(8,128)(2,1)} %get-tuple-element.12) | data formatting | bytes 589824
  34.5 5.6 %fusion.2 = f32[2,512,4,4,1]{3,2,4,1,0:T(4,128)S(1)} fusion(bf16[2,1,4,3,12,512]{4,2,3,5,0,1:T(4,128)(2,1)} %copy.83, bf16[2,1,4,3,12,512]{4,2,3,5,0,1:T(4,128)(2,1)S(1)} %copy.82), kind=kOutput, calls=%fused_computation.2 | convolution fusion | flops 1179648 | bytes 655360 | tf_op jit(solution)/shard_map/tscjn,tucjn->sutn/dot_general | solution.py:113
  40.2 5.0 %fusion = f32[2,512,4,4,1]{3,2,4,1,0:T(4,128)} fusion(bf16[2,1,4,3,12,512]{4,2,3,5,0,1:T(4,128)(2,1)S(1)} %copy-done.1, bf16[2,1,4,3,12,512]{4,2,3,5,0,1:T(4,128)(2,1)S(1)} %copy-done.2), kind=kOutput, calls=%fused_computation | convolution fusion | flops 1179648 | bytes 655360 | tf_op jit(solution)/shard_map/tscjn,tucjn->sutn/dot_general | solution.py:116
  45.2 3.7 %fusion.13 = f32[4,4,2,512]{0,1,3,2:T(4,128)} fusion(f32[2,512,4,4,1]{3,2,4,1,0:T(4,128)S(1)} %fusion.2, bf16[2,1,4,3,12,512]{4,2,3,5,0,1:T(4,128)(2,1)S(1)} %copy-done, bf16[2,1,4,3,12,512]{4,2,3,5,0,1:T(4,128)(2,1)S(1)} %copy-done.2), kind=kOutput, calls=%fused_computation.17 | convolution fusion | flops 1196032 | bytes 720896 | tf_op jit(solution)/shard_map/tscjn,tucjn->sutn/dot_general | solution.py:111
  48.8 2.1 copy.48
  51.0 7.5 %fusion.12 = f32[4,4,2,512]{0,1,3,2:T(4,128)} fusion(f32[2,512,4,4,1]{3,2,4,1,0:T(4,128)} %fusion, bf16[2,1,4,3,12,512]{4,2,3,5,0,1:T(4,128)(2,1)} %copy.81, bf16[2,1,4,3,12,512]{4,2,3,5,0,1:T(4,128)(2,1)S(1)} %copy.82), kind=kOutput, calls=%fused_computation.15 | convolution fusion | flops 1196032 | bytes 720896 | tf_op jit(solution)/shard_map/tscjn,tucjn->sutn/dot_general | solution.py:114
  58.5 1.9 copy.49
  60.5 0.7 fusion.146
  62.0 1.3 and_select_fusion.1
  65.5 0.7 pad_maximum_fusion
  66.3 0.6 iota_subtract_fusion
  67.0 0.7 add_subtract_fusion.1
  67.6 0.7 add_subtract_fusion
  68.7 1.1 add_sine_fusion
  70.0 0.7 and_select_fusion.3
  71.1 107.5 %all-gather.2.cloned.1.call-done = f32[32,2,2,64,64]{4,0,3,2,1:T(8,128)} async-done(((f32[32,2,2,4,64]{4,0,3,2,1:T(8,128)}), f32[32,2,2,64,64]{4,0,3,2,1:T(8,128)}) %all-gather.2.cloned.1.call-update) | async-done | bytes 2097168 | tf_op jit(solution)/shard_map/all_gather | solution.py:54
  178.6 4.7 %dynamic-slice_bitcast_fusion = (f32[32,2,64,4]{3,0,2,1:T(8,128)S(1)}, f32[32,2,64,4]{3,0,2,1:T(8,128)}) fusion(f32[32,2,2,64,64]{4,0,3,2,1:T(8,128)} %all-gather.2.cloned.1.call-done, s32[]{:T(128)S(6)} %add.213, s32[]{:T(128)S(6)} %select_n.88), kind=kLoop, calls=%fused_computation.12 | loop fusion | bytes 262152 | tf_op jit(solution)/shard_map/squeeze | solution.py:56
  183.3 2.6 copy.54
  186.9 1.2 copy.55
  189.4 1.0 reshape.373
  190.4 13.0 %all-to-all-start = ((f32[32,1,1024]{2,1,0:T(1,128)}), f32[32,1,1024]{2,1,0:T(1,128)S(1)}, u32[]{:S(2)}, u32[]{:S(2)}) async-start(f32[32,1,1024]{2,1,0:T(1,128)} %reshape.373), calls=%async_computation | async-start | bytes 262144 | tf_op jit(solution)/shard_map/all_to_all | solution.py:58
  203.8 106.2 %all-reduce = (f32[1,16,2,32]{3,2,1,0:T(2,128)S(1)}, f32[1,16,2,32]{3,2,1,0:T(2,128)S(1)}) all-reduce(f32[1,16,2,32]{3,2,1,0:T(2,128)S(1)} %bitcast.184, f32[1,16,2,32]{3,2,1,0:T(2,128)S(1)} %bitcast.183), channel_id=1, replica_groups=mesh['sx'=32,'sy'=16] {'sx','sy'}, use_global_device_ids=true, to_apply=%region_1.2 | all-reduce | flops 2048 | bytes 16384 | tf_op jit(solution)/shard_map/psum | solution.py:124
  311.1 0.9 reduce
  315.9 0.7 copy.65
  (61 shorter events, 11.7 us)
Async XLA Ops:
  7.2 171.4 %all-gather.2.cloned.1.call-start = ((), (), s32[]{:S(2)}) async-start(), calls=%async_computation.1 | async-start | bytes 4456448 | tf_op jit(solution)/shard_map/all_gather | solution.py:54
  34.5 5.6 %copy-start.1 = (bf16[2,1,4,3,12,512]{4,2,3,5,0,1:T(4,128)(2,1)S(1)}, bf16[2,1,4,3,12,512]{4,2,3,5,0,1:T(4,128)(2,1)}, u32[]{:S(2)}) copy-start(bf16[2,1,4,3,12,512]{4,2,3,5,0,1:T(4,128)(2,1)} %copy.83) | copy-start | bytes 884740
  34.5 5.6 %copy-start.2 = (bf16[2,1,4,3,12,512]{4,2,3,5,0,1:T(4,128)(2,1)S(1)}, bf16[2,1,4,3,12,512]{4,2,3,5,0,1:T(4,128)(2,1)}, u32[]{:S(2)}) copy-start(bf16[2,1,4,3,12,512]{4,2,3,5,0,1:T(4,128)(2,1)} %copy.80) | copy-start | bytes 884740
  40.2 5.0 %copy-start = (bf16[2,1,4,3,12,512]{4,2,3,5,0,1:T(4,128)(2,1)S(1)}, bf16[2,1,4,3,12,512]{4,2,3,5,0,1:T(4,128)(2,1)}, u32[]{:S(2)}) copy-start(bf16[2,1,4,3,12,512]{4,2,3,5,0,1:T(4,128)(2,1)} %copy.81) | copy-start | bytes 884740
  50.9 9.5 %copy-start.3 = (s32[3]{0:T(128)S(1)}, s32[3]{0:T(128)}, u32[]{:S(2)}) copy-start(s32[3]{0:T(128)} %param.8) | copy-start | bytes 40
  50.9 10.2 %slice-start = ((s32[16,4,2]{0,2,1:T(2,128)}), s32[16,4,1]{0,2,1:T(1,128)S(1)}, s32[]{:S(2)}) async-start(s32[16,4,2]{0,2,1:T(2,128)} %param.7), calls=%async_computation.2 | async-start | bytes 4096 | tf_op jit(solution)/shard_map/slice | solution.py:14
  58.5 9.8 %copy-start.4 = (s32[32,3]{0,1:T(4,128)S(1)}, s32[32,3]{0,1:T(4,128)}, u32[]{:S(2)}) copy-start(s32[32,3]{0,1:T(4,128)} %param.9) | copy-start | bytes 1156
  190.4 120.2 %all-to-all-start = ((f32[32,1,1024]{2,1,0:T(1,128)}), f32[32,1,1024]{2,1,0:T(1,128)S(1)}, u32[]{:S(2)}, u32[]{:S(2)}) async-start(f32[32,1,1024]{2,1,0:T(1,128)} %reshape.373), calls=%async_computation | async-start | bytes 262144 | tf_op jit(solution)/shard_map/all_to_all | solution.py:58
Sparse Core Ops, SparseCore 0:
  66.4 112.1 all-gather.1
where the time goes:
time: 325 us; the launch traced here: 323 us
  waiting for transfers between devices  108 us (33%)
  blocking collectives  106 us (33%)
  local copies, waits for them, and re-layouts  44.1 us (14%)
  matrix products  29.7 us (9%)
  between operations  14.4 us (4%)
  starting transfers between devices  13 us (4%)
  other arithmetic  8.45 us (3%)
    all_gather x1, waiting for transfers between devices, transform(): lax.all_gather(along_z, 'sy', axis=3, tiled=True)  107 us
    psum x1, blocking collectives, body(): listed_re, listed_im = lax.psum((local_re, local_im), ('sx', 'sy'))  106 us
    unnamed x19, local copies, waits for them, and re-layouts  20.8 us
    all_to_all x1, starting transfers between devices, transform(): lax.all_to_all(along_y, 'sx', split_axis=3, concat_axis=2, tiled=True)  13 us
    dot_general x1, matrix products, body(): jnp.einsum(pattern, backward[:, 0], forward[:, 1], preferred_element_type...  7.53 us
  transfers between devices with their start and end apart: 2, of which 1 were waited for; matrix products, arithmetic and copies ran while one was open for 2% of the time, Pallas kernels for 0%

commit v1 on v0

--- a/solution.py
+++ b/solution.py
@@ -51,7 +51,12 @@
     length_y = along_z.shape[3] * lax.axis_size("sy")
     full_re, full_im = dft_table(length_y, source_site[1])
     part = lax.dynamic_slice_in_dim(
-        lax.all_gather(along_z, "sy", axis=3, tiled=True), first_depth, depth_share, 4
+        jnp.concatenate(
+            lax.all_to_all(jnp.stack([along_z] * lax.axis_size("sy")), "sy", 0, 0), axis=3
+        ),
+        first_depth,
+        depth_share,
+        4,
     )
     step_re, step_im = complex_step(part[:, 0], part[:, 1], full_re, full_im, "nayc,yk->nakc")
     along_y = jnp.stack([step_re, step_im], 1)

time: 325 us -> 279 us (0.86)
  waiting for transfers between devices: 108 us -> 44.9 us
  between operations: 14.4 us -> 1.08 us
  starting transfers between devices: 13 us -> 25.8 us
  local copies, waits for them, and re-layouts: 44.1 us -> 56.9 us
  other arithmetic: 8.45 us -> 15.2 us
    all_gather x1 -> x0, waiting for transfers between devices: 107 us -> none  [transform(): lax.all_gather(along_z, 'sy', axis=3, tiled=True)]
    all_to_all x0 -> x1, waiting for transfers between devices: none -> 44.9 us  [transform(): lax.all_to_all(jnp.stack([along_z] * lax.axis_size('sy')), 'sy', 0, 0)]
    unnamed x19 -> x26, local copies, waits for them, and re-layouts: 20.8 us -> 36.9 us
    all_to_all x0 -> x1, starting transfers between devices: none -> 9.14 us  [transform(): lax.all_to_all(jnp.stack([along_z] * lax.axis_size('sy')), 'sy', 0, 0)]
    squeeze x3 -> x0, local copies, waits for them, and re-layouts: 8.52 us -> none  [the longest x2 5.88 us: transform(): part[:, 1]]
    all_to_all x0 -> x1, other arithmetic: none -> 7.32 us  [transform(): lax.all_to_all(jnp.stack([along_z] * lax.axis_size('sy')), 'sy', 0, 0)]
    all_to_all x1, starting transfers between devices: 13 us -> 16.7 us  [transform(): lax.all_to_all(along_y, 'sx', split_axis=3, concat_axis=2, tiled=True)]
    all_to_all x0 -> x2, local copies, waits for them, and re-layouts: none -> 3.26 us  [transform(): lax.all_to_all(jnp.stack([along_z] * lax.axis_size('sy')), 'sy', 0, 0)]
where the time goes in v1:
time: 279 us; the launch traced here: 278 us
  blocking collectives  104 us (37%)
  local copies, waits for them, and re-layouts  56.9 us (20%)
  waiting for transfers between devices  44.9 us (16%)
  matrix products  29.7 us (11%)
  starting transfers between devices  25.8 us (9%)
  other arithmetic  15.2 us (5%)
    psum x1, blocking collectives, body(): listed_re, listed_im = lax.psum((local_re, local_im), ('sx', 'sy'))  104 us
    all_to_all x1, waiting for transfers between devices, transform(): lax.all_to_all(jnp.stack([along_z] * lax.axis_size('sy')), 'sy', 0, 0)  44.9 us
    unnamed x26, local copies, waits for them, and re-layouts  36.9 us
    all_to_all x1, starting transfers between devices, transform(): lax.all_to_all(along_y, 'sx', split_axis=3, concat_axis=2, tiled=True)  16.7 us
    all_to_all x1, starting transfers between devices, transform(): lax.all_to_all(jnp.stack([along_z] * lax.axis_size('sy')), 'sy', 0, 0)  9.14 us
    dot_general x1, matrix products, body(): jnp.einsum(pattern, backward[:, 0], forward[:, 1], preferred_element_type...  7.53 us
    all_to_all x1, other arithmetic, transform(): lax.all_to_all(jnp.stack([along_z] * lax.axis_size('sy')), 'sy', 0, 0)  7.32 us
    dot_general x1, matrix products, body(): jnp.einsum(pattern, backward[:, 1], forward[:, 1], preferred_element_type...  5.64 us
  transfers between devices with their start and end apart: 2, of which 1 were waited for; matrix products, arithmetic and copies ran while one was open for 2% of the time, Pallas kernels for 0%

profile of v1, /device:TPU:1, one launch (start us, length us, event | category | flops | bytes accessed | tf_op | source)
XLA Modules:
  0.0 277.6 jit_solution(15155843826917794315)
XLA Ops:
  0.6 0.7 fusion.96
  1.3 2.1 reshape.381
  3.4 0.8 fusion.148
  4.3 4.5 %copy.74 = bf16[2,1,4,3,12,512]{4,2,3,5,0,1:T(4,128)(2,1)S(1)} copy(bf16[2,1,4,3,12,512]{5,4,3,2,1,0:T(8,128)(2,1)} %get-tuple-element.11) | data formatting | bytes 589824
  8.7 2.8 %reshape.382 = bf16[2,2,4,3,12,512]{5,4,3,2,1,0:T(8,128)(2,1)} reshape(bf16[2,2,12,12,2,256]{5,4,3,2,1,0:T(2,128)(2,1)} %param.6) | data formatting | bytes 1179648 | tf_op jit(solution)/shard_map/reshape | solution.py:114
  11.5 2.1 fusion.149
  13.6 5.2 %copy.75 = bf16[2,1,4,3,12,512]{4,2,3,5,0,1:T(4,128)(2,1)} copy(bf16[2,1,4,3,12,512]{5,4,3,2,1,0:T(8,128)(2,1)} %get-tuple-element.13) | data formatting | bytes 589824
  18.8 3.8 %copy.72 = bf16[2,1,4,3,12,512]{4,2,3,5,0,1:T(4,128)(2,1)} copy(bf16[2,1,4,3,12,512]{5,4,3,2,1,0:T(8,128)(2,1)S(1)} %get-tuple-element.10) | data formatting | bytes 589824
  22.6 5.3 %copy.73 = bf16[2,1,4,3,12,512]{4,2,3,5,0,1:T(4,128)(2,1)} copy(bf16[2,1,4,3,12,512]{5,4,3,2,1,0:T(8,128)(2,1)} %get-tuple-element.12) | data formatting | bytes 589824
  27.9 5.6 %fusion.2 = f32[2,512,4,4,1]{3,2,4,1,0:T(4,128)S(1)} fusion(bf16[2,1,4,3,12,512]{4,2,3,5,0,1:T(4,128)(2,1)} %copy.75, bf16[2,1,4,3,12,512]{4,2,3,5,0,1:T(4,128)(2,1)S(1)} %copy.74), kind=kOutput, calls=%fused_computation.2 | convolution fusion | flops 1179648 | bytes 655360 | tf_op jit(solution)/shard_map/tscjn,tucjn->sutn/dot_general | solution.py:118
  33.6 5.0 %fusion = f32[2,512,4,4,1]{3,2,4,1,0:T(4,128)} fusion(bf16[2,1,4,3,12,512]{4,2,3,5,0,1:T(4,128)(2,1)S(1)} %copy-done.2, bf16[2,1,4,3,12,512]{4,2,3,5,0,1:T(4,128)(2,1)S(1)} %copy-done.3), kind=kOutput, calls=%fused_computation | convolution fusion | flops 1179648 | bytes 655360 | tf_op jit(solution)/shard_map/tscjn,tucjn->sutn/dot_general | solution.py:121
  38.6 3.7 %fusion.13 = f32[4,4,2,512]{0,1,3,2:T(4,128)} fusion(f32[2,512,4,4,1]{3,2,4,1,0:T(4,128)S(1)} %fusion.2, bf16[2,1,4,3,12,512]{4,2,3,5,0,1:T(4,128)(2,1)S(1)} %copy-done.1, bf16[2,1,4,3,12,512]{4,2,3,5,0,1:T(4,128)(2,1)S(1)} %copy-done.3), kind=kOutput, calls=%fused_computation.15 | convolution fusion | flops 1196032 | bytes 720896 | tf_op jit(solution)/shard_map/tscjn,tucjn->sutn/dot_general | solution.py:116
  42.2 2.1 copy.42
  44.4 7.5 %fusion.12 = f32[4,4,2,512]{0,1,3,2:T(4,128)} fusion(f32[2,512,4,4,1]{3,2,4,1,0:T(4,128)} %fusion, bf16[2,1,4,3,12,512]{4,2,3,5,0,1:T(4,128)(2,1)} %copy.73, bf16[2,1,4,3,12,512]{4,2,3,5,0,1:T(4,128)(2,1)S(1)} %copy.74), kind=kOutput, calls=%fused_computation.13 | convolution fusion | flops 1196032 | bytes 720896 | tf_op jit(solution)/shard_map/tscjn,tucjn->sutn/dot_general | solution.py:119
  51.9 1.9 copy.43
  55.4 1.3 and_select_fusion.1
  59.0 2.5 broadcast_bitcast_fusion
  61.5 5.5 %reshape.383 = f32[16,1,32768]{2,1,0:T(1,128)} reshape(f32[16,2,2,4,32,64]{5,4,3,2,1,0:T(8,128)} %broadcast_bitcast_fusion) | data formatting | bytes 4194304
  67.0 9.1 %all-to-all-start = ((f32[16,1,32768]{2,1,0:T(1,128)}), f32[16,1,32768]{2,1,0:T(1,128)S(1)}, u32[]{:S(2)}, u32[]{:S(2)}) async-start(f32[16,1,32768]{2,1,0:T(1,128)} %reshape.383), calls=%async_computation | async-start | bytes 4194304 | tf_op jit(solution)/shard_map/all_to_all | solution.py:55
  78.6 1.1 add_sine_fusion
  81.0 44.9 %all-to-all-done = f32[16,1,32768]{2,1,0:T(1,128)S(1)} async-done(((f32[16,1,32768]{2,1,0:T(1,128)}), f32[16,1,32768]{2,1,0:T(1,128)S(1)}, u32[]{:S(2)}, u32[]{:S(2)}) %all-to-all-start) | async-done | bytes 2097184 | tf_op jit(solution)/shard_map/all_to_all | solution.py:55
  125.9 1.3 copy-done
  127.8 7.3 %reduce = f32[16,32768]{1,0:T(8,128)S(1)} reduce(f32[16,1,32768]{2,1,0:T(1,128)} %copy-done, f32[]{:T(128)} %broadcast.524), dimensions={1}, to_apply=%all_to_all.16.reduce_sub_computation | reduce | bytes 4194308 | tf_op jit(solution)/shard_map/all_to_all | solution.py:55
  135.1 3.0 %reshape.384 = f32[16,2,2,4,32,64]{5,4,3,2,1,0:T(8,128)} reshape(f32[16,32768]{1,0:T(8,128)S(1)} %reduce) | data formatting | bytes 4194304
  138.1 2.7 copy.48
  140.8 2.5 constant_dynamic-slice_fusion.1
  143.3 2.6 copy.77
  146.9 1.2 copy.78
  149.4 1.0 reshape.385
  150.4 16.7 %all-to-all-start.1 = ((f32[32,1,1024]{2,1,0:T(1,128)}), f32[32,1,1024]{2,1,0:T(1,128)S(1)}, u32[]{:S(2)}, u32[]{:S(2)}) async-start(f32[32,1,1024]{2,1,0:T(1,128)} %reshape.385), calls=%async_computation.1 | async-start | bytes 262144 | tf_op jit(solution)/shard_map/all_to_all | solution.py:63
  167.4 104.0 %all-reduce = (f32[1,16,2,32]{3,2,1,0:T(2,128)S(1)}, f32[1,16,2,32]{3,2,1,0:T(2,128)S(1)}) all-reduce(f32[1,16,2,32]{3,2,1,0:T(2,128)S(1)} %bitcast.194, f32[1,16,2,32]{3,2,1,0:T(2,128)S(1)} %bitcast.193), channel_id=1, replica_groups=mesh['sx'=32,'sy'=16] {'sx','sy'}, use_global_device_ids=true, to_apply=%region_1.2 | all-reduce | flops 2048 | bytes 16384 | tf_op jit(solution)/shard_map/psum | solution.py:129
  272.0 1.0 reduce.1
  (67 shorter events, 15.8 us)
Async XLA Ops:
  27.9 5.6 %copy-start.2 = (bf16[2,1,4,3,12,512]{4,2,3,5,0,1:T(4,128)(2,1)S(1)}, bf16[2,1,4,3,12,512]{4,2,3,5,0,1:T(4,128)(2,1)}, u32[]{:S(2)}) copy-start(bf16[2,1,4,3,12,512]{4,2,3,5,0,1:T(4,128)(2,1)} %copy.75) | copy-start | bytes 884740
  27.9 5.6 %copy-start.3 = (bf16[2,1,4,3,12,512]{4,2,3,5,0,1:T(4,128)(2,1)S(1)}, bf16[2,1,4,3,12,512]{4,2,3,5,0,1:T(4,128)(2,1)}, u32[]{:S(2)}) copy-start(bf16[2,1,4,3,12,512]{4,2,3,5,0,1:T(4,128)(2,1)} %copy.72) | copy-start | bytes 884740
  33.6 5.0 %copy-start.1 = (bf16[2,1,4,3,12,512]{4,2,3,5,0,1:T(4,128)(2,1)S(1)}, bf16[2,1,4,3,12,512]{4,2,3,5,0,1:T(4,128)(2,1)}, u32[]{:S(2)}) copy-start(bf16[2,1,4,3,12,512]{4,2,3,5,0,1:T(4,128)(2,1)} %copy.73) | copy-start | bytes 884740
  44.3 9.5 %copy-start.4 = (s32[3]{0:T(128)S(1)}, s32[3]{0:T(128)}, u32[]{:S(2)}) copy-start(s32[3]{0:T(128)} %param.8) | copy-start | bytes 40
  44.4 10.2 %slice-start = ((s32[16,4,2]{0,2,1:T(2,128)}), s32[16,4,1]{0,2,1:T(1,128)S(1)}, s32[]{:S(2)}) async-start(s32[16,4,2]{0,2,1:T(2,128)} %param.7), calls=%async_computation.2 | async-start | bytes 4096 | tf_op jit(solution)/shard_map/slice | solution.py:14
  67.0 11.2 %copy-start.5 = (s32[32,3]{0,1:T(4,128)S(1)}, s32[32,3]{0,1:T(4,128)}, u32[]{:S(2)}) copy-start(s32[32,3]{0,1:T(4,128)} %param.9) | copy-start | bytes 1156
  67.0 58.9 %all-to-all-start = ((f32[16,1,32768]{2,1,0:T(1,128)}), f32[16,1,32768]{2,1,0:T(1,128)S(1)}, u32[]{:S(2)}, u32[]{:S(2)}) async-start(f32[16,1,32768]{2,1,0:T(1,128)} %reshape.383), calls=%async_computation | async-start | bytes 4194304 | tf_op jit(solution)/shard_map/all_to_all | solution.py:55
  125.9 1.3 copy-start
  150.4 121.7 %all-to-all-start.1 = ((f32[32,1,1024]{2,1,0:T(1,128)}), f32[32,1,1024]{2,1,0:T(1,128)S(1)}, u32[]{:S(2)}, u32[]{:S(2)}) async-start(f32[32,1,1024]{2,1,0:T(1,128)} %reshape.385), calls=%async_computation.1 | async-start | bytes 262144 | tf_op jit(solution)/shard_map/all_to_all | solution.py:63
